TPU v7x, 512 devices: a whole 4x8x8 slice. The times are simulated.
512 devices in a mesh: row: 32 (over y_hi, z, core), col: 16 (over y_lo, x).
Axes of the slice: x: 4, y: 8 (y_hi: 2, y_lo: 4; y = y_hi * 4 + y_lo), z: 8, core: 2. Of those that a mesh axis runs over, the one named last changes fastest.
Arguments:
- stress: float32 [256, 16384], P('col', 'row'), may hold values from -2.5 to 2.5
- state: float32 [256, 8192], P('col', 'row'), may hold values from 0 to 1
- load_rate: int32 [256, 16384], P('col', 'row'), may hold values from 0 to 2047
- a_param: float32 [8192], P('row'), may hold values from 1 to 2
- b_param: float32 [8192], P('row'), may hold values from 0.25 to 1
- near_band: bfloat16 [16384, 768], P('row'), may hold values from -0.21875 to 0.21875
- u_far: bfloat16 [64, 64, 32, 256], P('row', 'col'), may hold values from -0.1875 to 0.1875
- v_far: bfloat16 [64, 64, 32, 256], P('row', 'col'), may hold values from -0.375 to 0.375
- ranks: int32 [64, 64], P('row', 'col'), may hold values from 1 to 32, as said below
Outputs:
- new_stress: float32 [256, 16384], P('col', 'row')
- new_state: float32 [256, 8192], P('col', 'row')
Inputs may be any that keep to these rules, and one draw needn't show every extreme that they name: ranks of blocks with |I - J| <= 1 are not used; blocks with |I - J| = 2 have rank 32.
All inputs are finite; a program needn't handle non-finite values.
Results may differ from a plain program's by a relative error of at most 0.0021.
Values may be sent and summed in bfloat16 or wider, within the bound.
No kernel may reach another device: no remote copies, remote signals or barrier semaphores. Data moves between devices by JAX's collectives and lax.ppermute only.
A program may use at most 64 MiB of HBM per device.

v0:
```python
import jax
import jax.numpy as jnp
from jax import lax
from jax.sharding import PartitionSpec as P

B = 128
HSTEP = 0.2
RATE_UNIT = 1.0 / 1024.0


def broadcast(value, axis, source):
    kept = jnp.where(lax.axis_index(axis) == source, value, 0).astype(value.dtype)
    return lax.psum(kept, axis)


def extended(cells, sides, width):
    for axis, dim in sides:
        count = lax.axis_size(axis)
        ends = count - 1
        head = lax.slice_in_dim(cells, 0, width, axis=dim)
        tail = lax.slice_in_dim(cells, cells.shape[dim] - width, cells.shape[dim], axis=dim)
        cells = jnp.concatenate(
            [
                lax.ppermute(tail, axis, [(i, (i + 1) % count) for i in range(ends)]),
                cells,
                lax.ppermute(head, axis, [((i + 1) % count, i) for i in range(ends)]),
            ],
            axis=dim,
        )
    return cells


def rates_and_drift(stress_now, state_now, plate_rate, a_param, b_param):
    members = stress_now.shape[0]
    block_count = a_param.shape[0] // B
    stress_view = stress_now.reshape(members, block_count, 2, B)
    state_view = state_now.reshape(members, block_count, 1, B)
    direct_view = a_param.reshape(1, block_count, 1, B)
    evolve_view = b_param.reshape(1, block_count, B)
    slip_rate = 2.0 * jnp.exp(-state_view) * jnp.sinh(stress_view / direct_view)
    slip_speed = jnp.sqrt(jnp.sum(slip_rate * slip_rate, axis=2))
    drift = evolve_view * (jnp.exp(-state_view[:, :, 0]) - slip_speed)
    excess = (slip_rate - plate_rate.reshape(members, block_count, 2, B)).astype(jnp.bfloat16)
    return (excess.reshape(members, -1), drift.reshape(members, -1))


def far_terms(columns, u_far, v_far, ranks, row_index, col_index):
    block_rows, block_cols, rank_slots, block_dofs = u_far.shape
    members = columns.shape[0]
    grid = columns.reshape(members, block_cols, block_dofs)
    weights = jnp.einsum("mjd,ijrd->ijmr", grid, v_far, preferred_element_type=jnp.float32)
    global_rows = row_index * block_rows + jnp.arange(block_rows, dtype=jnp.int32)
    global_cols = col_index * block_cols + jnp.arange(block_cols, dtype=jnp.int32)
    distant = jnp.abs(global_rows[:, None] - global_cols[None, :]) >= 2
    active = (jnp.arange(rank_slots, dtype=jnp.int32)[None, None, :] < ranks[:, :, None]) & distant[
        :, :, None
    ]
    weights = jnp.where(active[:, :, None, :], weights, 0.0).astype(jnp.bfloat16)
    partial_value = jnp.einsum("ijmr,ijrd->mid", weights, u_far, preferred_element_type=jnp.float32)
    return partial_value.reshape(members, -1)


def near_terms(padded, first_block, near_band):
    block_dofs = near_band.shape[1] // 3
    block_rows = near_band.shape[0] // block_dofs
    members = padded.shape[0]
    segment = lax.dynamic_slice_in_dim(
        padded, first_block * block_dofs, (block_rows + 2) * block_dofs, 1
    )
    segment = segment.reshape(members, block_rows + 2, block_dofs)
    windows = jnp.concatenate(
        [segment[:, 0:block_rows], segment[:, 1 : block_rows + 1], segment[:, 2 : block_rows + 2]],
        axis=2,
    )
    band_view = near_band.reshape(block_rows, block_dofs, 3 * block_dofs)
    nearby = jnp.einsum("mik,idk->mid", windows, band_view, preferred_element_type=jnp.float32)
    return nearby.reshape(members, -1)


def local(stress, state, load_rate, a_param, b_param, near_band, u_far, v_far, ranks):
    row_index = lax.axis_index("row")
    col_index = lax.axis_index("col")
    row_ratio = lax.axis_size("row") // lax.axis_size("col")
    block_rows = u_far.shape[0]
    block_dofs = near_band.shape[1] // 3
    plate_rate = load_rate.astype(jnp.float32) * RATE_UNIT
    stress_start, state_start = (stress, state)

    def tendency(stress_now, state_now):
        excess, drift = rates_and_drift(stress_now, state_now, plate_rate, a_param, b_param)
        all_members = lax.all_gather(excess, "col", axis=0, tiled=True)
        owners = []
        for offset in range(row_ratio):
            owners.append(broadcast(all_members, "row", row_ratio * col_index + offset))
        columns = jnp.concatenate(owners, axis=1)
        partial_value = far_terms(columns, u_far, v_far, ranks, row_index, col_index)
        padded = extended(columns, (("col", 1),), block_dofs)
        on_band = col_index == row_index // row_ratio
        first_block = row_index % row_ratio * block_rows
        partial_value = partial_value + lax.cond(
            on_band,
            lambda: near_terms(padded, first_block, near_band),
            lambda: jnp.zeros_like(partial_value),
        )
        totals = lax.psum_scatter(partial_value, "col", scatter_dimension=0, tiled=True)
        return (-totals, drift)

    rate_one, drift_one = tendency(stress_start, state_start)
    stress_one = stress_start + HSTEP * rate_one
    state_one = state_start + HSTEP * drift_one
    rate_two, drift_two = tendency(stress_one, state_one)
    stress_two = 0.75 * stress_start + 0.25 * (stress_one + HSTEP * rate_two)
    state_two = 0.75 * state_start + 0.25 * (state_one + HSTEP * drift_two)
    rate_three, drift_three = tendency(stress_two, state_two)
    new_stress = stress_start / 3.0 + 2.0 / 3.0 * (stress_two + HSTEP * rate_three)
    new_state = state_start / 3.0 + 2.0 / 3.0 * (state_two + HSTEP * drift_three)
    return (new_stress, new_state)


def solution(mesh):
    return jax.shard_map(
        local,
        mesh=mesh,
        in_specs=(
            P("col", "row"),
            P("col", "row"),
            P("col", "row"),
            P("row"),
            P("row"),
            P("row", None),
            P("row", "col", None, None),
            P("row", "col", None, None),
            P("row", "col"),
        ),
        out_specs=(P("col", "row"), P("col", "row")),
        check_vma=False,
    )
```

profile of v0, /device:TPU:64, one launch (start us, length us, event | category | flops | bytes accessed | tf_op | source)
XLA Modules:
  0.0 1475.0 jit_solution(9471608002866167742)
XLA Ops:
  7.2 0.7 fusion.75
  8.0 0.7 div.62
  8.7 0.8 fusion.59
  9.6 43.9 %all_gather.9 = bf16[256,512]{1,0:T(8,128)(2,1)S(1)} all-gather(bf16[16,512]{1,0:T(8,128)(2,1)S(1)} %fusion.59), channel_id=1, replica_groups=mesh['row'=32,'col'=16] {'col'}, dimensions={0}, use_global_device_ids=true | all-gather | bytes 278528 | tf_op jit(solution)/shard_map/all_gather | solution.py:91
  53.4 0.9 broadcast_select_fusion.5
  54.6 336.6 %all-reduce.11.cloned.1.call-done = (bf16[256,512]{1,0:T(8,128)(2,1)}, bf16[256,512]{1,0:T(8,128)(2,1)}) async-done(((bf16[256,512]{1,0:T(8,128)(2,1)}, bf16[256,512]{1,0:T(8,128)(2,1)}), (bf16[256,512]{1,0:T(8,128)(2,1)}, bf16[256,512]{1,0:T(8,128)(2,1)})) %all-reduce.11.cloned.1.call-update) | async-done | bytes 524304 | tf_op jit(solution)/shard_map/psum | solution.py:13
  391.1 0.9 slice.60
  392.1 0.9 slice.61
  393.0 1.1 pad_maximum_fusion.3
  394.1 3.4 collective-permute-start
  397.5 1.3 collective-permute-start.1
  398.8 0.4 reshape.192
  399.2 0.5 fusion.29
  399.9 0.6 collective-permute-done
  400.5 4.1 collective-permute-done.1
  404.9 0.9 add.112
  406.2 92.3 %reduce-scatter.4.cloned.1.call-done = f32[16,512]{1,0:T(8,128)} async-done(((f32[256,512]{1,0:T(8,128)}), f32[16,512]{1,0:T(8,128)}) %reduce-scatter.4.cloned.1.call-update) | async-done | bytes 32784 | tf_op jit(solution)/shard_map/reduce_scatter | solution.py:105
  498.5 0.8 fusion.58
  499.4 38.8 %all_gather.10 = bf16[256,512]{1,0:T(8,128)(2,1)S(1)} all-gather(bf16[16,512]{1,0:T(8,128)(2,1)S(1)} %get-tuple-element.58), channel_id=1, replica_groups=mesh['row'=32,'col'=16] {'col'}, dimensions={0}, use_global_device_ids=true | all-gather | bytes 278528 | tf_op jit(solution)/shard_map/all_gather | solution.py:91
  538.2 0.9 broadcast_select_fusion.4
  539.1 336.2 %all-reduce.9.cloned.1.call-done = (bf16[256,512]{1,0:T(8,128)(2,1)}, bf16[256,512]{1,0:T(8,128)(2,1)}) async-done(((bf16[256,512]{1,0:T(8,128)(2,1)}, bf16[256,512]{1,0:T(8,128)(2,1)}), (bf16[256,512]{1,0:T(8,128)(2,1)}, bf16[256,512]{1,0:T(8,128)(2,1)})) %all-reduce.9.cloned.1.call-update) | async-done | bytes 524304 | tf_op jit(solution)/shard_map/psum | solution.py:13
  875.3 0.9 slice.62
  876.2 0.9 slice.63
  877.1 1.1 pad_maximum_fusion.4
  878.2 3.4 collective-permute-start.2
  881.6 1.3 collective-permute-start.3
  882.9 0.4 reshape.194
  883.3 0.5 fusion.28
  884.0 0.7 collective-permute-done.2
  884.7 4.1 collective-permute-done.3
  888.9 0.9 add.115
  890.2 92.4 %reduce-scatter.6.cloned.1.call-done = f32[16,512]{1,0:T(8,128)} async-done(((f32[256,512]{1,0:T(8,128)}), f32[16,512]{1,0:T(8,128)}) %reduce-scatter.6.cloned.1.call-update) | async-done | bytes 32784 | tf_op jit(solution)/shard_map/reduce_scatter | solution.py:105
  982.7 0.8 fusion.57
  983.5 38.8 %all_gather.11 = bf16[256,512]{1,0:T(8,128)(2,1)S(1)} all-gather(bf16[16,512]{1,0:T(8,128)(2,1)S(1)} %get-tuple-element.56), channel_id=1, replica_groups=mesh['row'=32,'col'=16] {'col'}, dimensions={0}, use_global_device_ids=true | all-gather | bytes 278528 | tf_op jit(solution)/shard_map/all_gather | solution.py:91
  1022.3 0.9 broadcast_select_fusion.3
  1023.2 336.3 %all-reduce.7.cloned.1.call-done = (bf16[256,512]{1,0:T(8,128)(2,1)}, bf16[256,512]{1,0:T(8,128)(2,1)}) async-done(((bf16[256,512]{1,0:T(8,128)(2,1)}, bf16[256,512]{1,0:T(8,128)(2,1)}), (bf16[256,512]{1,0:T(8,128)(2,1)}, bf16[256,512]{1,0:T(8,128)(2,1)})) %all-reduce.7.cloned.1.call-update) | async-done | bytes 524304 | tf_op jit(solution)/shard_map/psum | solution.py:13
  1359.5 0.9 slice.64
  1360.5 0.9 slice.65
  1361.4 1.1 pad_maximum_fusion.5
  1362.5 3.4 collective-permute-start.4
  1365.9 1.3 collective-permute-start.5
  1367.5 0.5 fusion.27
  1368.3 0.7 collective-permute-done.4
  1368.9 4.1 collective-permute-done.5
  1373.2 0.9 add.120
  1374.3 0.6 fusion.64
  1375.0 91.8 %reduce-scatter.8.cloned.1.call-done = f32[16,512]{1,0:T(8,128)} async-done(((f32[256,512]{1,0:T(8,128)}), f32[16,512]{1,0:T(8,128)}) %reduce-scatter.8.cloned.1.call-update) | async-done | bytes 32784 | tf_op jit(solution)/shard_map/reduce_scatter | solution.py:105
  1466.7 1.4 multiply_add_fusion
  (79 shorter events, 2.9 us)
Async XLA Ops:
  7.2 392.0 %copy-start = (bf16[2,4,32,256]{3,2,1,0:T(8,128)(2,1)S(1)}, bf16[2,4,32,256]{3,2,1,0:T(8,128)(2,1)}, u32[]{:S(2)}) copy-start(bf16[2,4,32,256]{3,2,1,0:T(8,128)(2,1)} %param.21) | copy-start | bytes 393220
  7.2 384.0 %all-reduce.11.cloned.1.call-start = ((), (), s32[]{:S(2)}) async-start(), calls=%async_computation.8 | async-start | bytes 1048576 | tf_op jit(solution)/shard_map/psum | solution.py:13
  9.5 44.9 %copy-start.13 = (s32[2,4]{1,0:T(2,128)S(1)}, s32[2,4]{1,0:T(2,128)}, u32[]{:S(2)}) copy-start(s32[2,4]{1,0:T(2,128)} %param.23) | copy-start | bytes 100
  54.3 444.2 %reduce-scatter.4.cloned.1.call-start = ((), (), s32[]{:S(2)}) async-start(), calls=%async_computation.3 | async-start | bytes 557056 | tf_op jit(solution)/shard_map/reduce_scatter | solution.py:105
  393.0 6.2 copy-start.7
  394.1 6.4 collective-permute-start
  397.5 7.2 collective-permute-start.1
  399.7 5.0 copy-start.1
  399.7 5.0 copy-start.2
  399.9 4.8 copy-start.14
  404.8 1.0 copy-start.8
  404.8 1.0 copy-start.11
  404.8 1.2 copy-start.10
  404.9 1.2 copy-start.12
  405.8 92.8 %copy-start.9 = (s32[16,512]{1,0:T(8,128)S(1)}, s32[16,512]{1,0:T(8,128)}, u32[]{:S(2)}) copy-start(s32[16,512]{1,0:T(8,128)} %param.17) | copy-start | bytes 98308
  405.8 469.5 %all-reduce.9.cloned.1.call-start = ((), (), s32[]{:S(2)}) async-start(), calls=%async_computation.7 | async-start | bytes 1048576 | tf_op jit(solution)/shard_map/psum | solution.py:13
  539.1 443.6 %reduce-scatter.6.cloned.1.call-start = ((), (), s32[]{:S(2)}) async-start(), calls=%async_computation.4 | async-start | bytes 557056 | tf_op jit(solution)/shard_map/reduce_scatter | solution.py:105
  878.2 6.4 collective-permute-start.2
  881.6 7.2 collective-permute-start.3
  883.8 5.0 copy-start.5
  883.8 5.0 copy-start.6
  889.8 469.7 %all-reduce.7.cloned.1.call-start = ((), (), s32[]{:S(2)}) async-start(), calls=%async_computation.6 | async-start | bytes 1048576 | tf_op jit(solution)/shard_map/psum | solution.py:13
  1023.2 443.6 %reduce-scatter.8.cloned.1.call-start = ((), (), s32[]{:S(2)}) async-start(), calls=%async_computation.5 | async-start | bytes 557056 | tf_op jit(solution)/shard_map/reduce_scatter | solution.py:105
  1362.5 6.4 collective-permute-start.4
  1365.9 7.2 collective-permute-start.5
  1368.0 5.0 copy-start.3
  1368.0 5.0 copy-start.4
Sparse Core Ops, SparseCore 0:
  54.4 336.6 all-reduce.10
  405.9 92.5 reduce-scatter.3
  539.2 336.0 all-reduce.8
  890.0 92.6 reduce-scatter.5
  1023.3 336.2 all-reduce.6
  1374.2 92.4 reduce-scatter.7
where the time goes:
time: 1480 us; the launch traced here: 1470 us
  waiting for transfers between devices  1300 us (88%)
  blocking collectives  122 us (8%)
    psum x3, waiting for transfers between devices, broadcast(): return lax.psum(kept, axis)  1010 us
    reduce_scatter x3, waiting for transfers between devices, tendency(): lax.psum_scatter(partial_value, 'col', scatter_dimension=0, tiled=True)  277 us
    all_gather x3, blocking collectives, tendency(): all_members = lax.all_gather(excess, 'col', axis=0, tiled=True)  122 us
  transfers between devices with their start and end apart: 12, of which 12 were waited for; matrix products, arithmetic and copies ran while one was open for 0% of the time, Pallas kernels for 0%

commit v1 on v0

--- a/solution.py
+++ b/solution.py
@@ -6,6 +6,12 @@
 B = 128
 HSTEP = 0.2
 RATE_UNIT = 1.0 / 1024.0
+
+
+def make_members_all(arr_in):
+    carry = jnp.stack(lax.axis_size("col") * [arr_in], axis=0)
+    new = lax.all_to_all(carry, "col", 0, 0)
+    return jnp.concatenate(new, 0)
 
 
 def broadcast(value, axis, source):
@@ -88,7 +94,7 @@
 
     def tendency(stress_now, state_now):
         excess, drift = rates_and_drift(stress_now, state_now, plate_rate, a_param, b_param)
-        all_members = lax.all_gather(excess, "col", axis=0, tiled=True)
+        all_members = make_members_all(excess)
         owners = []
         for offset in range(row_ratio):
             owners.append(broadcast(all_members, "row", row_ratio * col_index + offset))

time: 1480 us -> 1400 us (0.946)
  blocking collectives: 122 us -> 25.7 us
    all_gather x3 -> x0, blocking collectives: 122 us -> none  [tendency(): all_members = lax.all_gather(excess, 'col', axis=0, tiled=True)]
    all_to_all x0 -> x2, blocking collectives: none -> 25.7 us  [make_members_all(): new = lax.all_to_all(carry, 'col', 0, 0)]
  transfers between devices with their start and end apart: 12 -> 13, of which waited for: 12 -> 13; matrix products, arithmetic and copies ran while one was open for 0% -> 0% of each run, Pallas kernels for 0% -> 0%
where the time goes in v1:
time: 1400 us
  waiting for transfers between devices  1310 us (94%)
  blocking collectives  25.7 us (2%)
  starting transfers between devices  21.8 us (2%)
  between operations  14.7 us (1%)
  other arithmetic  14.5 us (1%)
    psum x3, waiting for transfers between devices, broadcast(): return lax.psum(kept, axis)  1010 us
    reduce_scatter x3, waiting for transfers between devices, tendency(): lax.psum_scatter(partial_value, 'col', scatter_dimension=0, tiled=True)  277 us
  transfers between devices with their start and end apart: 13, of which 13 were waited for; matrix products, arithmetic and copies ran while one was open for 0% of the time, Pallas kernels for 0%

profile of v1, /device:TPU:64, one launch (start us, length us, event | category | flops | bytes accessed | tf_op | source)
XLA Modules:
  0.0 1396.7 jit_solution(2423876554976787005)
XLA Ops:
  7.2 0.8 fusion.69
  8.0 0.7 div.65
  8.7 0.8 fusion.53
  9.5 0.7 stack.9
  10.2 7.4 all-to-all-start
  17.8 10.6 all-to-all-done
  28.4 0.8 broadcast_select_fusion.5
  29.5 337.2 %all-reduce.11.cloned.1.call-done = (bf16[256,512]{1,0:T(8,128)(2,1)}, bf16[256,512]{1,0:T(8,128)(2,1)}) async-done(((bf16[256,512]{1,0:T(8,128)(2,1)}, bf16[256,512]{1,0:T(8,128)(2,1)}), (bf16[256,512]{1,0:T(8,128)(2,1)}, bf16[256,512]{1,0:T(8,128)(2,1)})) %all-reduce.11.cloned.1.call-update) | async-done | bytes 524304 | tf_op jit(solution)/shard_map/psum | solution.py:19
  366.7 0.9 slice.60
  367.6 0.9 slice.61
  368.5 1.1 pad_maximum_fusion.3
  369.6 3.5 collective-permute-start
  373.1 1.3 collective-permute-start.1
  374.7 0.4 fusion.29
  375.3 0.9 collective-permute-done
  376.2 4.1 collective-permute-done.1
  380.5 0.9 add.112
  381.8 92.4 %reduce-scatter.4.cloned.1.call-done = f32[16,512]{1,0:T(8,128)} async-done(((f32[256,512]{1,0:T(8,128)}), f32[16,512]{1,0:T(8,128)}) %reduce-scatter.4.cloned.1.call-update) | async-done | bytes 32784 | tf_op jit(solution)/shard_map/reduce_scatter | solution.py:111
  474.2 0.8 fusion.52
  475.1 12.8 all_to_all.15
  487.9 0.8 broadcast_select_fusion.4
  488.8 335.3 %all-reduce.9.cloned.1.call-done = (bf16[256,512]{1,0:T(8,128)(2,1)}, bf16[256,512]{1,0:T(8,128)(2,1)}) async-done(((bf16[256,512]{1,0:T(8,128)(2,1)}, bf16[256,512]{1,0:T(8,128)(2,1)}), (bf16[256,512]{1,0:T(8,128)(2,1)}, bf16[256,512]{1,0:T(8,128)(2,1)})) %all-reduce.9.cloned.1.call-update) | async-done | bytes 524304 | tf_op jit(solution)/shard_map/psum | solution.py:19
  824.1 0.9 slice.62
  825.1 0.9 slice.63
  826.0 1.1 pad_maximum_fusion.4
  827.1 3.4 collective-permute-start.2
  830.5 1.3 collective-permute-start.3
  832.0 0.4 fusion.28
  832.6 0.9 collective-permute-done.2
  833.5 4.1 collective-permute-done.3
  837.8 0.9 add.115
  839.1 92.4 %reduce-scatter.6.cloned.1.call-done = f32[16,512]{1,0:T(8,128)} async-done(((f32[256,512]{1,0:T(8,128)}), f32[16,512]{1,0:T(8,128)}) %reduce-scatter.6.cloned.1.call-update) | async-done | bytes 32784 | tf_op jit(solution)/shard_map/reduce_scatter | solution.py:111
  931.5 0.8 fusion.51
  932.4 12.8 all_to_all.16
  945.2 0.8 broadcast_select_fusion.3
  946.1 335.1 %all-reduce.7.cloned.1.call-done = (bf16[256,512]{1,0:T(8,128)(2,1)}, bf16[256,512]{1,0:T(8,128)(2,1)}) async-done(((bf16[256,512]{1,0:T(8,128)(2,1)}, bf16[256,512]{1,0:T(8,128)(2,1)}), (bf16[256,512]{1,0:T(8,128)(2,1)}, bf16[256,512]{1,0:T(8,128)(2,1)})) %all-reduce.7.cloned.1.call-update) | async-done | bytes 524304 | tf_op jit(solution)/shard_map/psum | solution.py:19
  1281.2 0.9 slice.64
  1282.1 0.9 slice.65
  1283.0 1.1 pad_maximum_fusion.5
  1284.1 3.4 collective-permute-start.4
  1287.5 1.3 collective-permute-start.5
  1289.0 0.4 fusion.27
  1289.6 0.9 collective-permute-done.4
  1290.5 4.1 collective-permute-done.5
  1294.8 0.9 add.120
  1295.9 0.6 fusion.58
  1296.6 91.8 %reduce-scatter.8.cloned.1.call-done = f32[16,512]{1,0:T(8,128)} async-done(((f32[256,512]{1,0:T(8,128)}), f32[16,512]{1,0:T(8,128)}) %reduce-scatter.8.cloned.1.call-update) | async-done | bytes 32784 | tf_op jit(solution)/shard_map/reduce_scatter | solution.py:111
  1388.4 1.4 multiply_add_fusion
  (87 shorter events, 3.2 us)
Async XLA Ops:
  7.2 367.5 %copy-start = (bf16[2,4,32,256]{3,2,1,0:T(8,128)(2,1)S(1)}, bf16[2,4,32,256]{3,2,1,0:T(8,128)(2,1)}, u32[]{:S(2)}) copy-start(bf16[2,4,32,256]{3,2,1,0:T(8,128)(2,1)} %param.21) | copy-start | bytes 393220
  10.2 18.1 %all-to-all-start = ((bf16[16,16,512]{2,1,0:T(8,128)(2,1)}), bf16[16,16,512]{2,1,0:T(8,128)(2,1)S(1)}, u32[]{:S(2)}, u32[]{:S(2)}) async-start(bf16[16,16,512]{2,1,0:T(8,128)(2,1)} %stack.9), calls=%async_computation | async-start | bytes 524288 | tf_op jit(solution)/shard_map/all_to_all | solution.py:13
  17.7 11.7 copy-start.13
  17.7 349.0 %all-reduce.11.cloned.1.call-start = ((), (), s32[]{:S(2)}) async-start(), calls=%async_computation.11 | async-start | bytes 1048576 | tf_op jit(solution)/shard_map/psum | solution.py:19
  29.2 445.0 %reduce-scatter.4.cloned.1.call-start = ((), (), s32[]{:S(2)}) async-start(), calls=%async_computation.6 | async-start | bytes 557056 | tf_op jit(solution)/shard_map/reduce_scatter | solution.py:111
  369.6 5.1 copy-start.7
  369.6 6.6 collective-permute-start
  373.1 7.2 collective-permute-start.1
  375.1 5.2 copy-start.1
  375.1 5.2 copy-start.2
  375.3 5.1 copy-start.14
  380.4 1.0 copy-start.8
  380.5 1.0 copy-start.11
  380.5 1.2 copy-start.10
  380.5 1.2 copy-start.12
  381.4 92.9 %copy-start.9 = (s32[16,512]{1,0:T(8,128)S(1)}, s32[16,512]{1,0:T(8,128)}, u32[]{:S(2)}) copy-start(s32[16,512]{1,0:T(8,128)} %param.17) | copy-start | bytes 98308
  381.4 442.7 %all-reduce.9.cloned.1.call-start = ((), (), s32[]{:S(2)}) async-start(), calls=%async_computation.10 | async-start | bytes 1048576 | tf_op jit(solution)/shard_map/psum | solution.py:19
  488.8 442.7 %reduce-scatter.6.cloned.1.call-start = ((), (), s32[]{:S(2)}) async-start(), calls=%async_computation.7 | async-start | bytes 557056 | tf_op jit(solution)/shard_map/reduce_scatter | solution.py:111
  827.1 6.4 collective-permute-start.2
  830.5 7.2 collective-permute-start.3
  832.4 5.3 copy-start.5
  832.4 5.2 copy-start.6
  832.6 5.1 copy-start.15
  838.7 442.5 %all-reduce.7.cloned.1.call-start = ((), (), s32[]{:S(2)}) async-start(), calls=%async_computation.9 | async-start | bytes 1048576 | tf_op jit(solution)/shard_map/psum | solution.py:19
  946.1 442.4 %reduce-scatter.8.cloned.1.call-start = ((), (), s32[]{:S(2)}) async-start(), calls=%async_computation.8 | async-start | bytes 557056 | tf_op jit(solution)/shard_map/reduce_scatter | solution.py:111
  1284.1 6.4 collective-permute-start.4
  1287.5 7.2 collective-permute-start.5
  1289.4 5.3 copy-start.3
  1289.4 5.2 copy-start.4
  1289.6 5.1 copy-start.16
Sparse Core Ops, SparseCore 0:
  29.4 337.2 all-reduce.10
  381.5 92.6 reduce-scatter.3
  488.9 335.1 all-reduce.8
  838.8 92.6 reduce-scatter.5
  946.2 334.9 all-reduce.6
  1295.8 92.5 reduce-scatter.7
